TPU v7x, 32 devices: a whole 2x2x4 slice. The times are simulated.
32 devices in a mesh: aux: 4 (over y, x), occ: 8 (over z, core).
Axes of the slice: x: 2, y: 2, z: 4, core: 2. Of those that a mesh axis runs over, the one named last changes fastest.
Arguments:
- factor: bfloat16 [6144, 8, 1536], P('aux', 'occ'), may hold values from -0.67578125 to 0.67578125
- occ_energy: float32 [1024], replicated, may hold values from -3 to -0.5
- vir_energy: float32 [3072], replicated, may hold values from 0.5 to 4
- occ_pick: int32 [8], replicated, may hold values from 0 to 1023
- vir_pick: int32 [1536], replicated, may hold values from 0 to 3071
Outputs:
- gamma: float32 [6144, 8, 1536], P('aux', 'occ')
All inputs are finite; a program needn't handle non-finite values.
Results may differ from a plain program's by a relative error of at most 0.0024.
Values may be sent and summed in bfloat16 or wider, within the bound.
No kernel may reach another device: no remote copies, remote signals or barrier semaphores. Data moves between devices by JAX's collectives and lax.ppermute only.
A program may use at most 192 MiB of HBM per device.

v0:
```python
import jax
import jax.numpy as jnp
from jax import lax
from jax.sharding import PartitionSpec as P


def shifted(block, axis, distance):
    devices = range(lax.axis_size(axis))
    route = [((i - distance) % len(devices), i) for i in devices]
    return lax.ppermute(block, axis, route)


def pair_density(left_block, right_block, pair_level, vir_levels, vir_rows):
    integrals = lax.psum_scatter(
        lax.dot_general(
            left_block, right_block, (((0,), (0,)), ((), ())), preferred_element_type=jnp.float32
        ),
        "aux",
        scatter_dimension=0,
        tiled=True,
    )
    divisor = pair_level - vir_rows[:, None] - vir_levels[None, :]
    amplitudes = (integrals / divisor).astype(jnp.bfloat16)
    return lax.dot_general(
        right_block,
        lax.all_gather(amplitudes, "aux", axis=0, tiled=True),
        (((1,), (1,)), ((), ())),
        preferred_element_type=jnp.float32,
    )


def on_device(factor, occ_energy, vir_energy, occ_pick, vir_pick):
    aux_count = lax.axis_size("aux")
    occ_count = lax.axis_size("occ")
    aux_place = lax.axis_index("aux")
    occ_place = lax.axis_index("occ")
    local_occ = factor.shape[1]
    virtuals = factor.shape[2]
    row_count = virtuals // aux_count
    occ_levels = jnp.take(occ_energy, occ_pick)
    vir_levels = jnp.take(vir_energy, vir_pick)
    row_start = aux_place * row_count
    vir_rows = lax.dynamic_slice_in_dim(vir_levels, row_start, row_count)
    near_block = shifted(factor, "occ", 1)
    far_block = shifted(near_block, "occ", 1)
    partners = ((1, near_block), (2, far_block))
    left_block = factor[:, 0, :]
    own_level = lax.dynamic_index_in_dim(occ_levels, occ_place * local_occ + 0, keepdims=False)
    density = jnp.zeros((factor.shape[0], virtuals), jnp.float32)
    for distance, block in partners:
        source_base = (occ_place - distance) % occ_count * local_occ
        right_block = block[:, 0, :]
        other_level = lax.dynamic_index_in_dim(occ_levels, source_base + 0, keepdims=False)
        density = density + pair_density(
            left_block, right_block, own_level + other_level, vir_levels, vir_rows
        )
    results = [density]
    return jnp.stack(results, axis=1)


def solution(mesh):
    placed = (P("aux", "occ", None), P(), P(), P(), P())
    return jax.shard_map(
        on_device, mesh=mesh, in_specs=placed, out_specs=P("aux", "occ", None), check_vma=False
    )
```

profile of v0, /device:TPU:0, one launch (start us, length us, event | category | flops | bytes accessed | tf_op | source)
XLA Modules:
  0.0 434.0 jit_solution(4172380707414738212)
XLA Ops:
  6.5 0.5 collective-permute-start
  7.0 56.0 %collective-permute-done = bf16[1536,1,1536]{2,0,1:T(8,128)(2,1)S(1)} collective-permute-done((bf16[1536,1,1536]{2,0,1:T(8,128)(2,1)}, bf16[1536,1,1536]{2,0,1:T(8,128)(2,1)S(1)}, u32[]{:S(2)}, u32[]{:S(2)}) %collective-permute-start) | collective-permute-done | bytes 4718624 | tf_op jit(solution)/shard_map/ppermute | solution.py:10
  63.1 2.1 copy-done.4
  65.2 11.6 %fusion.5 = f32[1536,1536]{1,0:T(8,128)} fusion(bf16[1536,1,1536]{2,0,1:T(8,128)(2,1)S(1)} %collective-permute-done, bf16[1536,1,1536]{2,0,1:T(8,128)(2,1)} %param.5), kind=kOutput, calls=%fused_computation.8 | convolution fusion | flops 7247757312 | bytes 18874368 | tf_op jit(solution)/shard_map/dot_general | solution.py:15
  76.8 0.1 collective-permute-start.1
  76.9 55.5 %collective-permute-done.1 = bf16[1536,1,1536]{2,0,1:T(8,128)(2,1)S(1)} collective-permute-done((bf16[1536,1,1536]{2,0,1:T(8,128)(2,1)}, bf16[1536,1,1536]{2,0,1:T(8,128)(2,1)S(1)}, u32[]{:S(2)}, u32[]{:S(2)}) %collective-permute-start.1) | collective-permute-done | bytes 4718624 | tf_op jit(solution)/shard_map/ppermute | solution.py:10
  132.5 2.2 copy-done.5
  134.7 11.6 %fusion.1 = f32[1536,1536]{1,0:T(8,128)} fusion(bf16[1536,1,1536]{2,0,1:T(8,128)(2,1)S(1)} %collective-permute-done.1, bf16[1536,1,1536]{2,0,1:T(8,128)(2,1)} %param.5), kind=kOutput, calls=%fused_computation.4 | convolution fusion | flops 7247757312 | bytes 18874368 | tf_op jit(solution)/shard_map/dot_general | solution.py:15
  146.3 0.0 all-gather.3.cloned.1.call-start
  146.4 0.5 copy-done.6
  147.0 0.6 gather_fusion
  147.6 0.7 fusion.9
  151.0 8.4 %gather_fusion.1 = f32[1536]{0:T(1024)S(1)} fusion(f32[3072]{0:T(1024)S(1)} %copy-done, s32[2048]{0:T(1024)S(1)} %pad_clamp_fusion), kind=kCustom, calls=%fused_computation.1 | custom fusion | bytes 18432 | tf_op jit(solution)/shard_map/jit(_take)/gather | solution.py:41
  159.4 0.1 dynamic-slice_subtract_fusion
  159.5 12.3 %reduce-scatter.3.cloned.1.call-done = f32[384,1536]{1,0:T(8,128)} async-done(((f32[1536,1536]{1,0:T(8,128)}), f32[384,1536]{1,0:T(8,128)}) %reduce-scatter.3.cloned.1.call-update) | async-done | bytes 2359312 | tf_op jit(solution)/shard_map/reduce_scatter | solution.py:14
  171.8 98.0 %reduce-scatter.5.cloned.1.call-done = f32[384,1536]{1,0:T(8,128)} async-done(((f32[1536,1536]{1,0:T(8,128)}), f32[384,1536]{1,0:T(8,128)}) %reduce-scatter.5.cloned.1.call-update) | async-done | bytes 2359312 | tf_op jit(solution)/shard_map/reduce_scatter | solution.py:14
  269.8 4.5 %divide_convert_fusion = (bf16[384,1536]{1,0:T(8,128)(2,1)}, bf16[384,1536]{1,0:T(8,128)(2,1)}) fusion(f32[384,1536]{1,0:T(8,128)} %reduce-scatter.5.cloned.1.call-done, f32[384]{0:T(512)S(1)} %get-tuple-element.7, f32[1536]{0:T(1024)S(1)} %and_select_fusion, f32[384,1536]{1,0:T(8,128)} %reduce-scatter.3.cloned.1.call-done, f32[384]{0:T(512)S(1)} %get-tuple-element.8), kind=kLoop, calls=%fused_computation.12 | loop fusion | flops 3538944 | bytes 7087104 | tf_op jit(solution)/shard_map/convert_element_type | solution.py:23
  274.3 0.2 all-gather.5.cloned.1.call-start
  274.5 0.3 all-gather.5.cloned.1.call-update
  274.9 56.5 %all-gather.3.cloned.1.call-done = bf16[1536,1536]{1,0:T(8,128)(2,1)} async-done(((bf16[384,1536]{1,0:T(8,128)(2,1)}), bf16[1536,1536]{1,0:T(8,128)(2,1)}) %all-gather.3.cloned.1.call-update) | async-done | bytes 4718608 | tf_op jit(solution)/shard_map/all_gather | solution.py:26
  331.4 13.0 %fusion.3 = f32[1536,1536]{1,0:T(8,128)} fusion(bf16[1536,1536]{1,0:T(8,128)(2,1)} %all-gather.3.cloned.1.call-done, bf16[1536,1,1536]{2,0,1:T(8,128)(2,1)} %copy-done.4), kind=kOutput, calls=%fused_computation.6 | convolution fusion | flops 7247757312 | bytes 18874368 | tf_op jit(solution)/shard_map/dot_general | solution.py:24
  344.4 45.7 %all-gather.5.cloned.1.call-done = bf16[1536,1536]{1,0:T(8,128)(2,1)} async-done(((bf16[384,1536]{1,0:T(8,128)(2,1)}), bf16[1536,1536]{1,0:T(8,128)(2,1)}) %all-gather.5.cloned.1.call-update) | async-done | bytes 4718608 | tf_op jit(solution)/shard_map/all_gather | solution.py:26
  390.1 14.5 %add_bitcast_fusion = f32[1536,1,1536]{0,2,1:T(8,128)} fusion(f32[1536,1536]{1,0:T(8,128)} %fusion.3, bf16[1536,1536]{1,0:T(8,128)(2,1)} %all-gather.5.cloned.1.call-done, bf16[1536,1,1536]{2,0,1:T(8,128)(2,1)} %copy-done.5), kind=kOutput, calls=%fused_computation.2 | convolution fusion | flops 7250116608 | bytes 28311552 | tf_op jit(solution)/shard_map/dot_general | solution.py:24
  404.5 22.9 %copy.7 = f32[1536,1,1536]{2,1,0:T(1,128)} copy(f32[1536,1,1536]{0,2,1:T(8,128)} %add_bitcast_fusion) | data formatting | bytes 18874368 | tf_op jit(solution)/shard_map/stack | solution.py:58
  (22 shorter events, 0.2 us)
Async XLA Ops:
  6.5 144.4 %copy-start = (f32[3072]{0:T(1024)S(1)}, f32[3072]{0:T(1024)}, u32[]{:S(2)}) copy-start(f32[3072]{0:T(1024)} %param.7) | copy-start | bytes 36868
  6.5 165.3 %reduce-scatter.3.cloned.1.call-start = ((), (), s32[]{:S(2)}) async-start(), calls=%async_computation.2 | async-start | bytes 11796480 | tf_op jit(solution)/shard_map/reduce_scatter | solution.py:14
  6.5 56.5 %collective-permute-start = (bf16[1536,1,1536]{2,0,1:T(8,128)(2,1)}, bf16[1536,1,1536]{2,0,1:T(8,128)(2,1)S(1)}, u32[]{:S(2)}, u32[]{:S(2)}) collective-permute-start(bf16[1536,1,1536]{2,0,1:T(8,128)(2,1)} %param.5), channel_id=1, source_target_pairs={{7,0},{0,1},{1,2},{2,3},{3,4},{4,5},{5,6},{6,7},{15,8},{8,9},{9,10... | collective-permute-start | bytes 14155784 | tf_op jit(solution)/shard_map/ppermute | solution.py:10
  63.1 2.1 copy-start.4
  76.8 193.0 %reduce-scatter.5.cloned.1.call-start = ((), (), s32[]{:S(2)}) async-start(), calls=%async_computation.4 | async-start | bytes 11796480 | tf_op jit(solution)/shard_map/reduce_scatter | solution.py:14
  76.8 55.6 %collective-permute-start.1 = (bf16[1536,1,1536]{2,0,1:T(8,128)(2,1)}, bf16[1536,1,1536]{2,0,1:T(8,128)(2,1)S(1)}, u32[]{:S(2)}, u32[]{:S(2)}) collective-permute-start(bf16[1536,1,1536]{2,0,1:T(8,128)(2,1)} %copy-done.4), channel_id=1, source_target_pairs={{7,0},{0,1},{1,2},{2,3},{3,4},{4,5},{5,6},{6,7},{15,8},{8,9},{9,10... | collective-permute-start | bytes 14155784 | tf_op jit(solution)/shard_map/ppermute | solution.py:10
  132.5 2.3 copy-start.5
  146.3 0.7 copy-start.6
  146.3 0.7 copy-start.2
  146.3 4.6 %copy-start.3 = (s32[1536]{0:T(1024)S(1)}, s32[1536]{0:T(1024)}, u32[]{:S(2)}) copy-start(s32[1536]{0:T(1024)} %param.9) | copy-start | bytes 18436
  146.3 185.1 %all-gather.3.cloned.1.call-start = ((), (), s32[]{:S(2)}) async-start(), calls=%async_computation.3 | async-start | bytes 5898240 | tf_op jit(solution)/shard_map/all_gather | solution.py:26
  274.3 115.7 %all-gather.5.cloned.1.call-start = ((), (), s32[]{:S(2)}) async-start(), calls=%async_computation.5 | async-start | bytes 5898240 | tf_op jit(solution)/shard_map/all_gather | solution.py:26
  404.5 22.9 %copy-start.1 = (f32[3072]{0:T(1024)S(1)}, f32[3072]{0:T(1024)}, u32[]{:S(2)}) copy-start(f32[3072]{0:T(1024)} %param.7) | copy-start | bytes 36868
Sparse Core Ops, SparseCore 0:
  76.9 94.8 reduce-scatter.2
  174.9 94.8 reduce-scatter.4
  274.4 56.9 all-gather.2
  333.1 56.9 all-gather.4
where the time goes:
time: 435 us; the launch traced here: 434 us
  waiting for transfers between devices  324 us (74%)
  matrix products  50.7 us (12%)
  local copies, waits for them, and re-layouts  37.5 us (9%)
  between operations  15.8 us (4%)
  other arithmetic  4.59 us (1%)
    ppermute x2, waiting for transfers between devices, shifted(): return lax.ppermute(block, axis, route)  112 us
    reduce_scatter x2, waiting for transfers between devices, pair_density(): lax.psum_scatter(lax.dot_general(left_block, right_block, (((0,), (0,)),...  110 us
    all_gather x2, waiting for transfers between devices, pair_density(): lax.all_gather(amplitudes, 'aux', axis=0, tiled=True)  102 us
    dot_general x2, matrix products, pair_density(): lax.dot_general(right_block, lax.all_gather(amplitudes, 'aux', axis=0, ti...  27.5 us
    dot_general x2, matrix products, pair_density(): lax.dot_general(left_block, right_block, (((0,), (0,)), ((), ())), prefer...  23.2 us
    another operation x1, local copies, waits for them, and re-layouts, on_device(): return jnp.stack(results, axis=1)  22.9 us
  transfers between devices with their start and end apart: 6, of which 6 were waited for; matrix products, arithmetic and copies ran while one was open for 8% of the time, Pallas kernels for 0%

commit v1 on v0

v1 whole, which is shorter than its diff:
```python
import jax
import jax.numpy as jnp
from jax import lax
from jax.experimental import pallas as pl
from jax.experimental.pallas import tpu as pltpu
from jax.sharding import PartitionSpec as P

LANES = 128
NEAR_SHARES = (2, 4, 6)
FAR_ORDER = (2, 1, 0)
GROUPS = ((0, 1), (2,), (3,), (4,), (5,))
TOP = 32768.0
VMEM_LIMIT = 24 << 20


def shifted(block, distance):
    size = lax.axis_size("occ")
    return lax.ppermute(block, "occ", [((i - distance) % size, i) for i in range(size)])


def swapped(block, bit):
    size = lax.axis_size("aux")
    return lax.ppermute(block, "aux", [(i, i ^ (1 << bit)) for i in range(size)])


def contract(left, right, dims):
    return lax.dot_general(left, right, (dims, ((), ())), preferred_element_type=jnp.float32)


def add_product(density, places, terms, linear):
    rows = terms[0][0].shape[0]
    part = terms[0][1][0].shape[0]
    count = len(terms[0][1])
    cols = part * count
    step = rows // 6 if rows % 96 == 0 else rows
    groups = cols // LANES

    def kernel(places_ref, *refs):
        refs = list(refs)
        density_ref = refs.pop(0) if density is not None else None
        term_refs = [(refs.pop(0), [refs.pop(0) for _ in range(count)]) for _ in terms]
        out_ref = refs.pop(0)
        full_ref = refs.pop(0) if linear else out_ref
        for q in range(count):
            spot = pl.ds(pl.multiple_of(places_ref[q], LANES), part)
            total = None
            for block_ref, piece_refs in term_refs:
                value = lax.dot_general(
                    block_ref[...], piece_refs[q][...], (((1,), (1,)), ((), ())), preferred_element_type=jnp.float32
                )
                total = value if total is None else total + value
            if density is not None:
                total = total + density_ref[:, spot]
            full_ref[:, spot] = total
        if linear:
            for g in range(groups):
                out_ref[pl.ds(g, step, stride=groups), :] = full_ref[:, g * LANES : (g + 1) * LANES]

    operands, in_specs = [], []
    if density is not None:
        operands.append(density)
        in_specs.append(pl.BlockSpec((step, cols), lambda r, _: (r, 0)))
    for block, pieces in terms:
        inner = block.shape[1]
        operands.append(block)
        in_specs.append(pl.BlockSpec((step, inner), lambda r, _: (r, 0)))
        for piece in pieces:
            operands.append(piece)
            in_specs.append(pl.BlockSpec((part, inner), lambda r, _: (0, 0)))
    if linear:
        out_shape = jax.ShapeDtypeStruct((rows * groups, LANES), jnp.float32)
        out_spec = pl.BlockSpec((step * groups, LANES), lambda r, _: (r, 0))
    else:
        out_shape = jax.ShapeDtypeStruct((rows, cols), jnp.float32)
        out_spec = pl.BlockSpec((step, cols), lambda r, _: (r, 0))
    return pl.pallas_call(
        kernel,
        grid_spec=pltpu.PrefetchScalarGridSpec(
            num_scalar_prefetch=1,
            grid=(rows // step,),
            in_specs=in_specs,
            out_specs=out_spec,
            scratch_shapes=[pltpu.VMEM((step, cols), jnp.float32)] if linear else [],
        ),
        out_shape=out_shape,
        compiler_params=pltpu.CompilerParams(vmem_limit_bytes=VMEM_LIMIT),
    )(places, *operands)


def on_device(factor, occ_energy, vir_energy, occ_pick, vir_pick):
    aux_count = lax.axis_size("aux")
    occ_count = lax.axis_size("occ")
    aux_place = lax.axis_index("aux")
    occ_place = lax.axis_index("occ")
    rows, _, virtuals = factor.shape
    bits = aux_count.bit_length() - 1
    own = factor[:, 0, :]

    unit = virtuals // sum(NEAR_SHARES)
    widths = [unit * s for s in NEAR_SHARES]
    starts = [sum(widths[:c]) for c in range(len(widths))]

    near = []
    source = own
    for c, (s, w) in enumerate(zip(starts, widths)):
        piece = lax.slice_in_dim(source, s, s + w, axis=1)
        if c == 0:
            source, piece = lax.optimization_barrier((source, piece))
        else:
            piece, _ = lax.optimization_barrier((piece, near[-1]))
        near.append(shifted(piece, 1))
    work = [(1, c, near[c]) for c in range(len(near))]
    work += [(2, c, shifted(near[c], 1)) for c in FAR_ORDER]


    half = virtuals // 2
    part = half // 2
    first_bits = (0, bits - 1)
    mine = [(aux_place >> b) & 1 for b in first_bits]
    keep_start = [h * half + mine[h] * part for h in range(2)]
    send_start = [h * half + (1 - mine[h]) * part for h in range(2)]
    places = jnp.stack([keep_start[0], send_start[0], keep_start[1], send_start[1]]).astype(jnp.int32)
    keep_left = [lax.dynamic_slice_in_dim(own, s, part, 1) for s in keep_start]
    send_left = [lax.dynamic_slice_in_dim(own, s, part, 1) for s in send_start]
    keep_left, send_left = lax.optimization_barrier((keep_left, send_left))
    first = [contract(send_left[h], near[0], ((0,), (0,))) for h in range(2)]
    occ_levels = jnp.take(occ_energy, occ_pick)
    vir_levels = jnp.take(vir_energy, vir_pick)
    keep_levels = [lax.dynamic_slice_in_dim(vir_levels, s, part) for s in keep_start]
    own_level = lax.dynamic_index_in_dim(occ_levels, occ_place, keepdims=False)

    top = jnp.max(jnp.abs(source)).astype(jnp.float32)
    top = jnp.full((8, LANES), top, jnp.float32)
    tops = jnp.stack([top, shifted(top, 1), shifted(top, 2)])
    for b in range(bits):
        tops = jnp.maximum(tops, swapped(tops, b))
    roots = jnp.minimum((TOP / (rows * aux_count)) ** 0.5 / jnp.maximum(tops[:, 0, 0], 1e-37), 1e18)
    scales = [roots[0] * roots[1], roots[0] * roots[2]]

    terms = []
    for k, (distance, c, block) in enumerate(work):
        other_level = lax.dynamic_index_in_dim(occ_levels, (occ_place - distance) % occ_count, keepdims=False)
        col_levels = lax.slice_in_dim(vir_levels, starts[c], starts[c] + widths[c])
        scale = scales[distance - 1]
        unscale = 1.0 / scale
        pieces = []
        for h in range(2):
            if k == 0:
                leaving = first[h]
            else:
                leaving = (contract(send_left[h], block, ((0,), (0,))) * scale).astype(jnp.float16)
            total = lax.optimization_barrier(contract(keep_left[h], block, ((0,), (0,))))
            row_levels, cols = keep_levels[h], col_levels
            route = [first_bits[h]] + [b for b in range(bits) if b != first_bits[h]]
            for stage, b in enumerate(route):
                if stage:
                    leaving = (total * scale).astype(jnp.float16) if k else total
                came = swapped(leaving, b)
                if stage == bits - 1:
                    came, row_levels, cols = lax.optimization_barrier((came, row_levels, cols))
                total = total + (came.astype(jnp.float32) * unscale if k else came)
            divisor = own_level + other_level - row_levels[:, None] - cols[None, :]
            kept = (total / divisor).astype(jnp.bfloat16)
            pieces += [kept, swapped(kept, first_bits[h])]
        terms.append((block, pieces))

    density = None
    for g, members in enumerate(GROUPS):
        last = g == len(GROUPS) - 1
        density = add_product(density, places, [terms[m] for m in members], last)
    return density.reshape(rows, 1, virtuals)


def solution(mesh):
    placed = (P("aux", "occ", None), P(), P(), P(), P())

    return jax.shard_map(
        on_device, mesh=mesh, in_specs=placed, out_specs=P("aux", "occ", None), check_vma=False
    )
```

time: 435 us -> 281 us (0.65)
  waiting for transfers between devices: 324 us -> 136 us
  starting transfers between devices: 0.86 us -> 43.3 us
  Pallas kernels: 0 us -> 30.9 us
  matrix products: 50.7 us -> 21.7 us
  between operations: 15.8 us -> 6.21 us
  other arithmetic: 4.59 us -> 9.92 us
  local copies, waits for them, and re-layouts: 37.5 us -> 32.5 us
    reduce_scatter x2 -> x0, waiting for transfers between devices: 110 us -> none  [pair_density(): lax.psum_scatter(lax.dot_general(left_block, right_block, (((0,), (0,)),...]
    all_gather x2 -> x0, waiting for transfers between devices: 102 us -> none  [pair_density(): lax.all_gather(amplitudes, 'aux', axis=0, tiled=True)]
    ppermute x2 -> x46, starting transfers between devices: 0.55 us -> 43.3 us  [the longest x38 38.2 us: swapped(): return lax.ppermute(block, 'aux', [(i, i ^ 1 << bit) for i in range(size)])]
    pallas_call x0 -> x5, Pallas kernels: none -> 30.9 us  [add_product(): pl.pallas_call(kernel, grid_spec=pltpu.PrefetchScalarGridSpec(num_scalar_...]
    dot_general x4 -> x24, matrix products: 50.7 us -> 21.7 us  [contract(): lax.dot_general(left, right, (dims, ((), ())), preferred_element_type=jnp...]
    ppermute x2 -> x46, waiting for transfers between devices: 112 us -> 136 us  [the longest x38 121 us: swapped(): return lax.ppermute(block, 'aux', [(i, i ^ 1 << bit) for i in range(size)])]
    another operation x1, local copies, waits for them, and re-layouts: 22.9 us -> 0.01 us  [on_device(): tops = jnp.stack([top, shifted(top, 1), shifted(top, 2)])]
    slice x0 -> x7, local copies, waits for them, and re-layouts: none -> 8.25 us  [the longest x3 7.11 us: on_device(): piece = lax.slice_in_dim(source, s, s + w, axis=1)]
  transfers between devices with their start and end apart: 6 -> 46, of which waited for: 6 -> 27; matrix products, arithmetic and copies ran while one was open for 8% -> 17% of each run, Pallas kernels for 0% -> 9%
where the time goes in v1:
time: 281 us
  waiting for transfers between devices  136 us (48%)
  starting transfers between devices  43.3 us (15%)
  local copies, waits for them, and re-layouts  32.5 us (12%)
  Pallas kernels  30.9 us (11%)
  matrix products  21.7 us (8%)
  other arithmetic  9.92 us (4%)
  between operations  6.21 us (2%)
    ppermute x38, waiting for transfers between devices, swapped(): return lax.ppermute(block, 'aux', [(i, i ^ 1 << bit) for i in range(size)])  121 us
    ppermute x38, starting transfers between devices, swapped(): return lax.ppermute(block, 'aux', [(i, i ^ 1 << bit) for i in range(size)])  38.2 us
    pallas_call x5, Pallas kernels, add_product(): pl.pallas_call(kernel, grid_spec=pltpu.PrefetchScalarGridSpec(num_scalar_...  30.9 us
    dot_general x24, matrix products, contract(): lax.dot_general(left, right, (dims, ((), ())), preferred_element_type=jnp...  21.7 us
    ppermute x8, waiting for transfers between devices, shifted(): lax.ppermute(block, 'occ', [((i - distance) % size, i) for i in range(siz...  14.9 us
    unnamed x30, local copies, waits for them, and re-layouts  9.56 us
    gather x1, local copies, waits for them, and re-layouts, on_device(): vir_levels = jnp.take(vir_energy, vir_pick)  8.39 us
    slice x3, local copies, waits for them, and re-layouts, on_device(): piece = lax.slice_in_dim(source, s, s + w, axis=1)  7.11 us
  transfers between devices with their start and end apart: 46, of which 27 were waited for; matrix products, arithmetic and copies ran while one was open for 17% of the time, Pallas kernels for 9%

profile of v1, /device:TPU:0, one launch (start us, length us, event | category | flops | bytes accessed | tf_op | source)
XLA Modules:
  0.0 280.6 jit_solution(4191613428994152002)
XLA Ops:
  10.3 8.4 %gather_fusion = f32[1536]{0:T(1024)S(1)} fusion(f32[3072]{0:T(1024)S(1)} %copy-done, s32[2048]{0:T(1024)S(1)} %pad_clamp_fusion), kind=kCustom, calls=%fused_computation | custom fusion | bytes 18432 | tf_op jit(solution)/shard_map/jit(_take)/gather | solution.py:128
  18.7 4.3 %dynamic-slice_bitcast_fusion = (bf16[1536,384]{1,0:T(8,128)(2,1)}, bf16[1536,384]{1,0:T(8,128)(2,1)S(1)}, bf16[1536,384]{1,0:T(8,128)(2,1)}, bf16[1536,384]{1,0:T(8,128)(2,1)}) fusion(bf16[1536,1,1536]{2,0,1:T(8,128)(2,1)} %param.5, s32[]{:T(128)S(6)} %select_n.68, s32[]{:T(128)S(6)} %select_n.66, s32[]{:T(128)S(6)} %select_n.65, s32[]{:T(128)S(6)} %select_n.67), kind=kLoop, calls=%fused_computation.33 | loop fusion | bytes 9437200 | tf_op jit(solution)/shard_map/dynamic_slice | solution.py:124
  45.0 5.8 %collective-permute-done.1 = f32[384,256]{1,0:T(8,128)S(1)} collective-permute-done((f32[384,256]{1,0:T(8,128)S(1)}, f32[384,256]{1,0:T(8,128)S(1)}, u32[]{:S(2)}, u32[]{:S(2)}) %collective-permute-start.1) | collective-permute-done | bytes 393248 | tf_op jit(solution)/shard_map/ppermute | solution.py:23
  63.6 6.3 %collective-permute-done.5 = f32[384,256]{1,0:T(8,128)S(1)} collective-permute-done((f32[384,256]{1,0:T(8,128)S(1)}, f32[384,256]{1,0:T(8,128)S(1)}, u32[]{:S(2)}, u32[]{:S(2)}) %collective-permute-start.5) | collective-permute-done | bytes 393248 | tf_op jit(solution)/shard_map/ppermute | solution.py:23
  74.6 4.0 %collective-permute-done.40 = f16[384,256]{1,0:T(8,128)(2,1)S(1)} collective-permute-done((f16[384,256]{1,0:T(8,128)(2,1)S(1)}, f16[384,256]{1,0:T(8,128)(2,1)S(1)}, u32[]{:S(2)}, u32[]{:S(2)}) %collective-permute-start.40) | collective-permute-done | bytes 196640 | tf_op jit(solution)/shard_map/ppermute | solution.py:23
  93.3 5.1 %collective-permute-done.12 = f16[384,512]{1,0:T(8,128)(2,1)S(1)} collective-permute-done((f16[384,512]{1,0:T(8,128)(2,1)S(1)}, f16[384,512]{1,0:T(8,128)(2,1)S(1)}, u32[]{:S(2)}, u32[]{:S(2)}) %collective-permute-start.12) | collective-permute-done | bytes 393248 | tf_op jit(solution)/shard_map/ppermute | solution.py:23
  102.8 5.7 %collective-permute-done.13 = f16[384,512]{1,0:T(8,128)(2,1)S(1)} collective-permute-done((f16[384,512]{1,0:T(8,128)(2,1)S(1)}, f16[384,512]{1,0:T(8,128)(2,1)S(1)}, u32[]{:S(2)}, u32[]{:S(2)}) %collective-permute-start.13) | collective-permute-done | bytes 393248 | tf_op jit(solution)/shard_map/ppermute | solution.py:23
  110.7 4.2 %collective-permute-done.32.refs_1_ = bf16[1536,512]{1,0:T(8,128)(2,1)S(1)} collective-permute-done((bf16[1536,512]{1,0:T(8,128)(2,1)S(1)}, bf16[1536,512]{1,0:T(8,128)(2,1)S(1)}, u32[]{:S(2)}, u32[]{:S(2)}) %collective-permute-start.32) | collective-permute-done | bytes 1572896 | tf_op jit(solution)/shard_map/ppermute | solution.py:18
  120.2 3.9 %collective-permute-done.33 = f16[384,512]{1,0:T(8,128)(2,1)S(1)} collective-permute-done((f16[384,512]{1,0:T(8,128)(2,1)S(1)}, f16[384,512]{1,0:T(8,128)(2,1)S(1)}, u32[]{:S(2)}, u32[]{:S(2)}) %collective-permute-start.33) | collective-permute-done | bytes 393248 | tf_op jit(solution)/shard_map/ppermute | solution.py:23
  125.5 3.9 %collective-permute-done.36 = f16[384,512]{1,0:T(8,128)(2,1)S(1)} collective-permute-done((f16[384,512]{1,0:T(8,128)(2,1)S(1)}, f16[384,512]{1,0:T(8,128)(2,1)S(1)}, u32[]{:S(2)}, u32[]{:S(2)}) %collective-permute-start.36) | collective-permute-done | bytes 393248 | tf_op jit(solution)/shard_map/ppermute | solution.py:23
  129.6 10.7 %collective-permute-done.18.refs_1_ = bf16[1536,768]{1,0:T(8,128)(2,1)S(1)} collective-permute-done((bf16[1536,768]{1,0:T(8,128)(2,1)S(1)}, bf16[1536,768]{1,0:T(8,128)(2,1)S(1)}, u32[]{:S(2)}, u32[]{:S(2)}) %collective-permute-start.18) | collective-permute-done | bytes 2359328 | tf_op jit(solution)/shard_map/ppermute | solution.py:18
  147.5 10.1 %collective-permute-done.19 = f16[384,768]{1,0:T(8,128)(2,1)S(1)} collective-permute-done((f16[384,768]{1,0:T(8,128)(2,1)S(1)}, f16[384,768]{1,0:T(8,128)(2,1)S(1)}, u32[]{:S(2)}, u32[]{:S(2)}) %collective-permute-start.19) | collective-permute-done | bytes 589856 | tf_op jit(solution)/shard_map/ppermute | solution.py:23
  163.8 10.4 %collective-permute-done.20 = f16[384,768]{1,0:T(8,128)(2,1)S(1)} collective-permute-done((f16[384,768]{1,0:T(8,128)(2,1)S(1)}, f16[384,768]{1,0:T(8,128)(2,1)S(1)}, u32[]{:S(2)}, u32[]{:S(2)}) %collective-permute-start.20) | collective-permute-done | bytes 589856 | tf_op jit(solution)/shard_map/ppermute | solution.py:23
  183.8 12.4 %collective-permute-done.26 = f16[384,768]{1,0:T(8,128)(2,1)S(1)} collective-permute-done((f16[384,768]{1,0:T(8,128)(2,1)S(1)}, f16[384,768]{1,0:T(8,128)(2,1)S(1)}, u32[]{:S(2)}, u32[]{:S(2)}) %collective-permute-start.26) | collective-permute-done | bytes 589856 | tf_op jit(solution)/shard_map/ppermute | solution.py:23
  200.0 11.1 %collective-permute-done.27 = f16[384,768]{1,0:T(8,128)(2,1)S(1)} collective-permute-done((f16[384,768]{1,0:T(8,128)(2,1)S(1)}, f16[384,768]{1,0:T(8,128)(2,1)S(1)}, u32[]{:S(2)}, u32[]{:S(2)}) %collective-permute-start.27) | collective-permute-done | bytes 589856 | tf_op jit(solution)/shard_map/ppermute | solution.py:23
  218.2 4.9 %collective-permute-done.17.refs_9_ = bf16[384,512]{1,0:T(8,128)(2,1)S(1)} collective-permute-done((bf16[384,512]{1,0:T(8,128)(2,1)S(1)}, bf16[384,512]{1,0:T(8,128)(2,1)S(1)}, u32[]{:S(2)}, u32[]{:S(2)}) %collective-permute-start.17) | collective-permute-done | bytes 393248 | tf_op jit(solution)/shard_map/ppermute | solution.py:23
  223.4 5.7 %collective-permute-done.21.refs_3_ = bf16[384,768]{1,0:T(8,128)(2,1)S(1)} collective-permute-done((bf16[384,768]{1,0:T(8,128)(2,1)S(1)}, bf16[384,768]{1,0:T(8,128)(2,1)S(1)}, u32[]{:S(2)}, u32[]{:S(2)}) %collective-permute-start.21) | collective-permute-done | bytes 589856 | tf_op jit(solution)/shard_map/ppermute | solution.py:23
  229.6 6.2 %collective-permute-done.24.refs_5_ = bf16[384,768]{1,0:T(8,128)(2,1)S(1)} collective-permute-done((bf16[384,768]{1,0:T(8,128)(2,1)S(1)}, bf16[384,768]{1,0:T(8,128)(2,1)S(1)}, u32[]{:S(2)}, u32[]{:S(2)}) %collective-permute-start.24) | collective-permute-done | bytes 589856 | tf_op jit(solution)/shard_map/ppermute | solution.py:23
  236.0 5.7 %collective-permute-done.28.refs_3_ = bf16[384,768]{1,0:T(8,128)(2,1)S(1)} collective-permute-done((bf16[384,768]{1,0:T(8,128)(2,1)S(1)}, bf16[384,768]{1,0:T(8,128)(2,1)S(1)}, u32[]{:S(2)}, u32[]{:S(2)}) %collective-permute-start.28) | collective-permute-done | bytes 589856 | tf_op jit(solution)/shard_map/ppermute | solution.py:23
  242.1 6.7 %shard_map.55.refs_0_ = f32[1536,1536]{1,0:T(8,128)S(1)} custom-call(s32[4]{0:T(128)S(1)} %pad_add_fusion.places_ref, bf16[1536,256]{1,0:T(8,128)(2,1)S(1)} %collective-permute-done.refs_0_, bf16[384,256]{1,0:T(8,128)(2,1)S(1)} %divide_convert_fusion.11.refs_1_, bf16[384,256]{1,0:T(8,128)(2,1)S(1)} %collective-permute-done.3.refs_2_, ...), custom_call_target="tpu_custom_call" | custom-call | tf_op jit(solution)/shard_map/pallas_call | solution.py:76
  256.2 6.5 %shard_map.56.refs_0_ = f32[1536,1536]{1,0:T(8,128)S(1)} custom-call(s32[4]{0:T(128)S(1)} %pad_add_fusion.places_ref, f32[1536,1536]{1,0:T(8,128)S(1)} %copy-done.3, bf16[1536,768]{1,0:T(8,128)(2,1)S(1)} %collective-permute-done.18.refs_1_, bf16[384,768]{1,0:T(8,128)(2,1)S(1)} %divide_convert_fusion.3.refs_2_, ...), custom_call_target="tpu_custom_call" | custom-call | tf_op jit(solution)/shard_map/pallas_call | solution.py:76
  262.8 6.5 %shard_map.57.refs_0_ = f32[1536,1536]{1,0:T(8,128)S(1)} custom-call(s32[4]{0:T(128)S(1)} %pad_add_fusion.places_ref, f32[1536,1536]{1,0:T(8,128)S(1)} %shard_map.56.refs_0_, bf16[1536,768]{1,0:T(8,128)(2,1)S(1)} %collective-permute-done.25.refs_1_, bf16[384,768]{1,0:T(8,128)(2,1)S(1)} %divide_convert_fusion.1.refs_2_, ...), custom_call_target="tpu_custom_call" | custom-call | tf_op jit(solution)/shard_map/pallas_call | solution.py:76
  269.4 5.0 %shard_map.58.refs_0_ = f32[1536,1536]{1,0:T(8,128)S(1)} custom-call(s32[4]{0:T(128)S(1)} %pad_add_fusion.places_ref, f32[1536,1536]{1,0:T(8,128)S(1)} %shard_map.57.refs_0_, bf16[1536,512]{1,0:T(8,128)(2,1)S(1)} %collective-permute-done.32.refs_1_, bf16[384,512]{1,0:T(8,128)(2,1)S(1)} %divide_convert_fusion.5.refs_2_, ...), custom_call_target="tpu_custom_call" | custom-call | tf_op jit(solution)/shard_map/pallas_call | solution.py:76
  274.4 6.2 %shard_map.59 = f32[18432,128]{1,0:T(8,128)} custom-call(s32[4]{0:T(128)S(1)} %pad_add_fusion.places_ref, f32[1536,1536]{1,0:T(8,128)S(1)} %shard_map.58.refs_0_, bf16[1536,256]{1,0:T(8,128)(2,1)S(1)} %collective-permute-done.39.refs_1_, bf16[384,256]{1,0:T(8,128)(2,1)S(1)} %divide_convert_fusion.9.refs_2_, ...), custom_call_target="tpu_custom_call" | custom-call | tf_op jit(solution)/shard_map/pallas_call | solution.py:76
  (188 shorter events, 114.5 us)
Async XLA Ops:
  5.4 18.9 %collective-permute-start.9 = (f32[8,128]{1,0:T(8,128)S(1)}, f32[8,128]{1,0:T(8,128)S(1)}, u32[]{:S(2)}, u32[]{:S(2)}) collective-permute-start(f32[8,128]{1,0:T(8,128)S(1)} %broadcast_in_dim.17), channel_id=1, source_target_pairs={{6,0},{7,1},{0,2},{1,3},{2,4},{3,5},{4,6},{5,7},{14,8},{15,9},{8,1... | collective-permute-start | bytes 12296 | tf_op jit(solution)/shard_map/ppermute | solution.py:18
  8.5 30.7 %collective-permute-start = (bf16[1536,256]{1,0:T(8,128)(2,1)S(1)}, bf16[1536,256]{1,0:T(8,128)(2,1)S(1)}, u32[]{:S(2)}, u32[]{:S(2)}) collective-permute-start(bf16[1536,256]{1,0:T(8,128)(2,1)S(1)} %slice.51), channel_id=1, source_target_pairs={{7,0},{0,1},{1,2},{2,3},{3,4},{4,5},{5,6},{6,7},{15,8},{8,9},{9,10... | collective-permute-start | bytes 2359304 | tf_op jit(solution)/shard_map/ppermute | solution.py:18
  45.0 24.9 %collective-permute-start.39 = (bf16[1536,256]{1,0:T(8,128)(2,1)S(1)}, bf16[1536,256]{1,0:T(8,128)(2,1)S(1)}, u32[]{:S(2)}, u32[]{:S(2)}) collective-permute-start(bf16[1536,256]{1,0:T(8,128)(2,1)S(1)} %collective-permute-done.refs_0_), channel_id=1, source_target_pairs={{7,0},{0,1},{1,2},{2,3},{3,4},{4,5},{5,6},{6,7},{15,8},{8,9},{9,10... | collective-permute-start | bytes 2359304 | tf_op jit(solution)/shard_map/ppermute | solution.py:18
  56.1 31.7 %collective-permute-start.7 = (bf16[1536,512]{1,0:T(8,128)(2,1)S(1)}, bf16[1536,512]{1,0:T(8,128)(2,1)S(1)}, u32[]{:S(2)}, u32[]{:S(2)}) collective-permute-start(bf16[1536,512]{1,0:T(8,128)(2,1)S(1)} %copy-done.11), channel_id=1, source_target_pairs={{7,0},{0,1},{1,2},{2,3},{3,4},{4,5},{5,6},{6,7},{15,8},{8,9},{9,10... | collective-permute-start | bytes 4718600 | tf_op jit(solution)/shard_map/ppermute | solution.py:18
  62.6 151.0 %collective-permute-start.3 = (bf16[384,256]{1,0:T(8,128)(2,1)S(1)}, bf16[384,256]{1,0:T(8,128)(2,1)S(1)}, u32[]{:S(2)}, u32[]{:S(2)}) collective-permute-start(bf16[384,256]{1,0:T(8,128)(2,1)S(1)} %divide_convert_fusion.11.refs_1_), channel_id=1, source_target_pairs={{0,8},{8,0},{16,24},{24,16},{1,9},{9,1},{17,25},{25,17},{2,10},{10... | collective-permute-start | bytes 589832 | tf_op jit(solution)/shard_map/ppermute | solution.py:23
  93.3 21.7 %collective-permute-start.32 = (bf16[1536,512]{1,0:T(8,128)(2,1)S(1)}, bf16[1536,512]{1,0:T(8,128)(2,1)S(1)}, u32[]{:S(2)}, u32[]{:S(2)}) collective-permute-start(bf16[1536,512]{1,0:T(8,128)(2,1)S(1)} %collective-permute-done.7.refs_5_), channel_id=1, source_target_pairs={{7,0},{0,1},{1,2},{2,3},{3,4},{4,5},{5,6},{6,7},{15,8},{8,9},{9,10... | collective-permute-start | bytes 4718600 | tf_op jit(solution)/shard_map/ppermute | solution.py:18
  102.6 37.7 %collective-permute-start.18 = (bf16[1536,768]{1,0:T(8,128)(2,1)S(1)}, bf16[1536,768]{1,0:T(8,128)(2,1)S(1)}, u32[]{:S(2)}, u32[]{:S(2)}) collective-permute-start(bf16[1536,768]{1,0:T(8,128)(2,1)S(1)} %copy-done.10), channel_id=1, source_target_pairs={{7,0},{0,1},{1,2},{2,3},{3,4},{4,5},{5,6},{6,7},{15,8},{8,9},{9,10... | collective-permute-start | bytes 7077896 | tf_op jit(solution)/shard_map/ppermute | solution.py:18
  124.3 22.6 %collective-permute-start.34 = (f16[384,512]{1,0:T(8,128)(2,1)S(1)}, f16[384,512]{1,0:T(8,128)(2,1)S(1)}, u32[]{:S(2)}, u32[]{:S(2)}) collective-permute-start(f16[384,512]{1,0:T(8,128)(2,1)S(1)} %multiply_convert_fusion.5), channel_id=1, source_target_pairs={{0,16},{8,24},{16,0},{24,8},{1,17},{9,25},{17,1},{25,9},{2,18},{10... | collective-permute-start | bytes 1179656 | tf_op jit(solution)/shard_map/ppermute | solution.py:23
  141.4 16.3 %collective-permute-start.19 = (f16[384,768]{1,0:T(8,128)(2,1)S(1)}, f16[384,768]{1,0:T(8,128)(2,1)S(1)}, u32[]{:S(2)}, u32[]{:S(2)}) collective-permute-start(f16[384,768]{1,0:T(8,128)(2,1)S(1)} %fusion), channel_id=1, source_target_pairs={{0,8},{8,0},{16,24},{24,16},{1,9},{9,1},{17,25},{25,17},{2,10},{10... | collective-permute-start | bytes 1769480 | tf_op jit(solution)/shard_map/ppermute | solution.py:23
  144.1 32.2 %collective-permute-start.25 = (bf16[1536,768]{1,0:T(8,128)(2,1)S(1)}, bf16[1536,768]{1,0:T(8,128)(2,1)S(1)}, u32[]{:S(2)}, u32[]{:S(2)}) collective-permute-start(bf16[1536,768]{1,0:T(8,128)(2,1)S(1)} %collective-permute-done.18.refs_1_), channel_id=1, source_target_pairs={{7,0},{0,1},{1,2},{2,3},{3,4},{4,5},{5,6},{6,7},{15,8},{8,9},{9,10... | collective-permute-start | bytes 7077896 | tf_op jit(solution)/shard_map/ppermute | solution.py:18
  145.3 16.3 %collective-permute-start.22 = (f16[384,768]{1,0:T(8,128)(2,1)S(1)}, f16[384,768]{1,0:T(8,128)(2,1)S(1)}, u32[]{:S(2)}, u32[]{:S(2)}) collective-permute-start(f16[384,768]{1,0:T(8,128)(2,1)S(1)} %fusion.1), channel_id=1, source_target_pairs={{0,16},{8,24},{16,0},{24,8},{1,17},{9,25},{17,1},{25,9},{2,18},{10... | collective-permute-start | bytes 1769480 | tf_op jit(solution)/shard_map/ppermute | solution.py:23
  157.9 16.3 %collective-permute-start.20 = (f16[384,768]{1,0:T(8,128)(2,1)S(1)}, f16[384,768]{1,0:T(8,128)(2,1)S(1)}, u32[]{:S(2)}, u32[]{:S(2)}) collective-permute-start(f16[384,768]{1,0:T(8,128)(2,1)S(1)} %multiply_convert_fusion.3), channel_id=1, source_target_pairs={{0,16},{8,24},{16,0},{24,8},{1,17},{9,25},{17,1},{25,9},{2,18},{10... | collective-permute-start | bytes 1769480 | tf_op jit(solution)/shard_map/ppermute | solution.py:23
  162.9 51.0 %collective-permute-start.6 = (bf16[384,256]{1,0:T(8,128)(2,1)S(1)}, bf16[384,256]{1,0:T(8,128)(2,1)S(1)}, u32[]{:S(2)}, u32[]{:S(2)}) collective-permute-start(bf16[384,256]{1,0:T(8,128)(2,1)S(1)} %divide_convert_fusion.10.refs_3_), channel_id=1, source_target_pairs={{0,16},{8,24},{16,0},{24,8},{1,17},{9,25},{17,1},{25,9},{2,18},{10... | collective-permute-start | bytes 589832 | tf_op jit(solution)/shard_map/ppermute | solution.py:23
  174.2 41.9 %collective-permute-start.14 = (bf16[384,512]{1,0:T(8,128)(2,1)S(1)}, bf16[384,512]{1,0:T(8,128)(2,1)S(1)}, u32[]{:S(2)}, u32[]{:S(2)}) collective-permute-start(bf16[384,512]{1,0:T(8,128)(2,1)S(1)} %divide_convert_fusion.7.refs_6_), channel_id=1, source_target_pairs={{0,8},{8,0},{16,24},{24,16},{1,9},{9,1},{17,25},{25,17},{2,10},{10... | collective-permute-start | bytes 1179656 | tf_op jit(solution)/shard_map/ppermute | solution.py:23
  178.6 17.7 %collective-permute-start.26 = (f16[384,768]{1,0:T(8,128)(2,1)S(1)}, f16[384,768]{1,0:T(8,128)(2,1)S(1)}, u32[]{:S(2)}, u32[]{:S(2)}) collective-permute-start(f16[384,768]{1,0:T(8,128)(2,1)S(1)} %fusion.2), channel_id=1, source_target_pairs={{0,8},{8,0},{16,24},{24,16},{1,9},{9,1},{17,25},{25,17},{2,10},{10... | collective-permute-start | bytes 1769480 | tf_op jit(solution)/shard_map/ppermute | solution.py:23
  182.3 16.3 %collective-permute-start.29 = (f16[384,768]{1,0:T(8,128)(2,1)S(1)}, f16[384,768]{1,0:T(8,128)(2,1)S(1)}, u32[]{:S(2)}, u32[]{:S(2)}) collective-permute-start(f16[384,768]{1,0:T(8,128)(2,1)S(1)} %fusion.3), channel_id=1, source_target_pairs={{0,16},{8,24},{16,0},{24,8},{1,17},{9,25},{17,1},{25,9},{2,18},{10... | collective-permute-start | bytes 1769480 | tf_op jit(solution)/shard_map/ppermute | solution.py:23
  212.9 16.2 %collective-permute-start.21 = (bf16[384,768]{1,0:T(8,128)(2,1)S(1)}, bf16[384,768]{1,0:T(8,128)(2,1)S(1)}, u32[]{:S(2)}, u32[]{:S(2)}) collective-permute-start(bf16[384,768]{1,0:T(8,128)(2,1)S(1)} %divide_convert_fusion.3.refs_2_), channel_id=1, source_target_pairs={{0,8},{8,0},{16,24},{24,16},{1,9},{9,1},{17,25},{25,17},{2,10},{10... | collective-permute-start | bytes 1769480 | tf_op jit(solution)/shard_map/ppermute | solution.py:23
  213.6 22.2 %collective-permute-start.24 = (bf16[384,768]{1,0:T(8,128)(2,1)S(1)}, bf16[384,768]{1,0:T(8,128)(2,1)S(1)}, u32[]{:S(2)}, u32[]{:S(2)}) collective-permute-start(bf16[384,768]{1,0:T(8,128)(2,1)S(1)} %divide_convert_fusion.2.refs_4_), channel_id=1, source_target_pairs={{0,16},{8,24},{16,0},{24,8},{1,17},{9,25},{17,1},{25,9},{2,18},{10... | collective-permute-start | bytes 1769480 | tf_op jit(solution)/shard_map/ppermute | solution.py:23
  214.0 27.7 %collective-permute-start.28 = (bf16[384,768]{1,0:T(8,128)(2,1)S(1)}, bf16[384,768]{1,0:T(8,128)(2,1)S(1)}, u32[]{:S(2)}, u32[]{:S(2)}) collective-permute-start(bf16[384,768]{1,0:T(8,128)(2,1)S(1)} %divide_convert_fusion.1.refs_2_), channel_id=1, source_target_pairs={{0,8},{8,0},{16,24},{24,16},{1,9},{9,1},{17,25},{25,17},{2,10},{10... | collective-permute-start | bytes 1769480 | tf_op jit(solution)/shard_map/ppermute | solution.py:23
  216.1 46.6 %collective-permute-start.31 = (bf16[384,768]{1,0:T(8,128)(2,1)S(1)}, bf16[384,768]{1,0:T(8,128)(2,1)S(1)}, u32[]{:S(2)}, u32[]{:S(2)}) collective-permute-start(bf16[384,768]{1,0:T(8,128)(2,1)S(1)} %divide_convert_fusion.refs_4_), channel_id=1, source_target_pairs={{0,16},{8,24},{16,0},{24,8},{1,17},{9,25},{17,1},{25,9},{2,18},{10... | collective-permute-start | bytes 1769480 | tf_op jit(solution)/shard_map/ppermute | solution.py:23
  223.1 46.2 %collective-permute-start.35 = (bf16[384,512]{1,0:T(8,128)(2,1)S(1)}, bf16[384,512]{1,0:T(8,128)(2,1)S(1)}, u32[]{:S(2)}, u32[]{:S(2)}) collective-permute-start(bf16[384,512]{1,0:T(8,128)(2,1)S(1)} %divide_convert_fusion.5.refs_2_), channel_id=1, source_target_pairs={{0,8},{8,0},{16,24},{24,16},{1,9},{9,1},{17,25},{25,17},{2,10},{10... | collective-permute-start | bytes 1179656 | tf_op jit(solution)/shard_map/ppermute | solution.py:23
  229.1 40.2 %collective-permute-start.38 = (bf16[384,512]{1,0:T(8,128)(2,1)S(1)}, bf16[384,512]{1,0:T(8,128)(2,1)S(1)}, u32[]{:S(2)}, u32[]{:S(2)}) collective-permute-start(bf16[384,512]{1,0:T(8,128)(2,1)S(1)} %divide_convert_fusion.4.refs_4_), channel_id=1, source_target_pairs={{0,16},{8,24},{16,0},{24,8},{1,17},{9,25},{17,1},{25,9},{2,18},{10... | collective-permute-start | bytes 1179656 | tf_op jit(solution)/shard_map/ppermute | solution.py:23
  235.8 38.5 %collective-permute-start.42 = (bf16[384,256]{1,0:T(8,128)(2,1)S(1)}, bf16[384,256]{1,0:T(8,128)(2,1)S(1)}, u32[]{:S(2)}, u32[]{:S(2)}) collective-permute-start(bf16[384,256]{1,0:T(8,128)(2,1)S(1)} %divide_convert_fusion.9.refs_2_), channel_id=1, source_target_pairs={{0,8},{8,0},{16,24},{24,16},{1,9},{9,1},{17,25},{25,17},{2,10},{10... | collective-permute-start | bytes 589832 | tf_op jit(solution)/shard_map/ppermute | solution.py:23
  241.7 32.6 %collective-permute-start.45 = (bf16[384,256]{1,0:T(8,128)(2,1)S(1)}, bf16[384,256]{1,0:T(8,128)(2,1)S(1)}, u32[]{:S(2)}, u32[]{:S(2)}) collective-permute-start(bf16[384,256]{1,0:T(8,128)(2,1)S(1)} %divide_convert_fusion.8.refs_4_), channel_id=1, source_target_pairs={{0,16},{8,24},{16,0},{24,8},{1,17},{9,25},{17,1},{25,9},{2,18},{10... | collective-permute-start | bytes 589832 | tf_op jit(solution)/shard_map/ppermute | solution.py:23
  (37 other events, 314.1 us)

commit v2 on v1

--- a/solution.py
+++ b/solution.py
@@ -21,6 +21,11 @@
 def swapped(block, bit):
     size = lax.axis_size("aux")
     return lax.ppermute(block, "aux", [(i, i ^ (1 << bit)) for i in range(size)])
+
+
+def picked(values, picks):
+    spots = lax.broadcasted_iota(jnp.int32, (values.shape[0], picks.shape[0]), 0)
+    return jnp.sum(jnp.where(spots == picks[None, :], values[:, None], 0.0), axis=0)
 
 
 def contract(left, right, dims):
@@ -102,13 +107,13 @@
 
     near = []
     source = own
+    room = (TOP / (rows * aux_count)) ** 0.5
     for c, (s, w) in enumerate(zip(starts, widths)):
         piece = lax.slice_in_dim(source, s, s + w, axis=1)
         if c == 0:
             source, piece = lax.optimization_barrier((source, piece))
-        else:
-            piece, _ = lax.optimization_barrier((piece, near[-1]))
         near.append(shifted(piece, 1))
+
     work = [(1, c, near[c]) for c in range(len(near))]
     work += [(2, c, shifted(near[c], 1)) for c in FAR_ORDER]
 
@@ -123,19 +128,18 @@
     keep_left = [lax.dynamic_slice_in_dim(own, s, part, 1) for s in keep_start]
     send_left = [lax.dynamic_slice_in_dim(own, s, part, 1) for s in send_start]
     keep_left, send_left = lax.optimization_barrier((keep_left, send_left))
+    top = jnp.full((8, LANES), jnp.max(jnp.abs(source)), jnp.float32)
+    for b in range(bits):
+        top = jnp.maximum(top, swapped(top, b))
+    root = jnp.minimum(room / jnp.maximum(top, 1e-37), 1e18)
+    partner_roots = [shifted(root, d) for d in (1, 2)]
+    scales = [(root * other)[0, 0] for other in partner_roots]
+
     first = [contract(send_left[h], near[0], ((0,), (0,))) for h in range(2)]
-    occ_levels = jnp.take(occ_energy, occ_pick)
-    vir_levels = jnp.take(vir_energy, vir_pick)
+    occ_levels = picked(occ_energy, occ_pick)
+    vir_levels = picked(vir_energy, vir_pick)
     keep_levels = [lax.dynamic_slice_in_dim(vir_levels, s, part) for s in keep_start]
     own_level = lax.dynamic_index_in_dim(occ_levels, occ_place, keepdims=False)
-
-    top = jnp.max(jnp.abs(source)).astype(jnp.float32)
-    top = jnp.full((8, LANES), top, jnp.float32)
-    tops = jnp.stack([top, shifted(top, 1), shifted(top, 2)])
-    for b in range(bits):
-        tops = jnp.maximum(tops, swapped(tops, b))
-    roots = jnp.minimum((TOP / (rows * aux_count)) ** 0.5 / jnp.maximum(tops[:, 0, 0], 1e-37), 1e18)
-    scales = [roots[0] * roots[1], roots[0] * roots[2]]
 
     terms = []
     for k, (distance, c, block) in enumerate(work):
@@ -174,6 +178,4 @@
 def solution(mesh):
     placed = (P("aux", "occ", None), P(), P(), P(), P())
 
-    return jax.shard_map(
-        on_device, mesh=mesh, in_specs=placed, out_specs=P("aux", "occ", None), check_vma=False
-    )
+    return jax.shard_map(on_device, mesh=mesh, in_specs=placed, out_specs=P("aux", "occ", None), check_vma=False)

time: 281 us -> 275 us (0.979)
  waiting for transfers between devices: 136 us -> 104 us
  matrix products: 21.7 us -> 35.7 us
  other arithmetic: 9.92 us -> 21.4 us
  local copies, waits for them, and re-layouts: 32.5 us -> 21.4 us
  starting transfers between devices: 43.3 us -> 53 us
  Pallas kernels: 30.9 us -> 33.9 us
    ppermute x38, waiting for transfers between devices: 121 us -> 78.7 us  [swapped(): return lax.ppermute(block, 'aux', [(i, i ^ 1 << bit) for i in range(size)])]
    dot_general x24, matrix products: 21.7 us -> 35.7 us  [contract(): lax.dot_general(left, right, (dims, ((), ())), preferred_element_type=jnp...]
    ppermute x8, waiting for transfers between devices: 14.9 us -> 24.9 us  [shifted(): lax.ppermute(block, 'occ', [((i - distance) % size, i) for i in range(siz...]
    gather x2 -> x0, local copies, waits for them, and re-layouts: 9.02 us -> none  [the longest x1 8.39 us: on_device(): vir_levels = jnp.take(vir_energy, vir_pick)]
    ppermute x38, starting transfers between devices: 38.2 us -> 46.1 us  [swapped(): return lax.ppermute(block, 'aux', [(i, i ^ 1 << bit) for i in range(size)])]
    convert_element_type x10, other arithmetic: 1.71 us -> 8.25 us  [on_device(): leaving = (total * scale).astype(jnp.float16) if k else total]
    unnamed x30 -> x46, local copies, waits for them, and re-layouts: 9.56 us -> 4.52 us
    reduce_sum x0 -> x2, other arithmetic: none -> 3.33 us  [picked(): jnp.sum(jnp.where(spots == picks[None, :], values[:, None], 0.0), axis=0)]
  transfers between devices with their start and end apart: 46 -> 46, of which waited for: 27 -> 20; matrix products, arithmetic and copies ran while one was open for 17% -> 26% of each run, Pallas kernels for 9% -> 10%
where the time goes in v2:
time: 275 us; the launch traced here: 274 us
  waiting for transfers between devices  104 us (38%)
  starting transfers between devices  53 us (19%)
  matrix products  35.7 us (13%)
  Pallas kernels  33.9 us (12%)
  local copies, waits for them, and re-layouts  21.4 us (8%)
  other arithmetic  21.4 us (8%)
  between operations  5.08 us (2%)
    ppermute x38, waiting for transfers between devices, swapped(): return lax.ppermute(block, 'aux', [(i, i ^ 1 << bit) for i in range(size)])  78.7 us
    ppermute x38, starting transfers between devices, swapped(): return lax.ppermute(block, 'aux', [(i, i ^ 1 << bit) for i in range(size)])  46.1 us
    dot_general x24, matrix products, contract(): lax.dot_general(left, right, (dims, ((), ())), preferred_element_type=jnp...  35.7 us
    pallas_call x5, Pallas kernels, add_product(): pl.pallas_call(kernel, grid_spec=pltpu.PrefetchScalarGridSpec(num_scalar_...  33.9 us
    ppermute x8, waiting for transfers between devices, shifted(): lax.ppermute(block, 'occ', [((i - distance) % size, i) for i in range(siz...  24.9 us
    convert_element_type x10, other arithmetic, on_device(): leaving = (total * scale).astype(jnp.float16) if k else total  8.25 us
    slice x3, local copies, waits for them, and re-layouts, on_device(): piece = lax.slice_in_dim(source, s, s + w, axis=1)  8.11 us
    ppermute x8, starting transfers between devices, shifted(): lax.ppermute(block, 'occ', [((i - distance) % size, i) for i in range(siz...  6.85 us
  transfers between devices with their start and end apart: 46, of which 20 were waited for; matrix products, arithmetic and copies ran while one was open for 26% of the time, Pallas kernels for 10%

profile of v2, /device:TPU:0, one launch (start us, length us, event | category | flops | bytes accessed | tf_op | source)
XLA Modules:
  0.0 274.1 jit_solution(17967603469800696810)
XLA Ops:
  14.1 4.3 %dynamic-slice_bitcast_fusion = (bf16[1536,384]{1,0:T(8,128)(2,1)}, bf16[1536,384]{1,0:T(8,128)(2,1)S(1)}, bf16[1536,384]{1,0:T(8,128)(2,1)}, bf16[1536,384]{1,0:T(8,128)(2,1)}) fusion(bf16[1536,1,1536]{2,0,1:T(8,128)(2,1)} %param.5, s32[]{:T(128)S(6)} %select_n.58, s32[]{:T(128)S(6)} %select_n.56, s32[]{:T(128)S(6)} %select_n.55, s32[]{:T(128)S(6)} %select_n.57), kind=kLoop, calls=%fused_computation.33 | loop fusion | bytes 9437200 | tf_op jit(solution)/shard_map/dynamic_slice | solution.py:129
  26.3 7.8 %collective-permute-done.1 = f32[384,256]{1,0:T(8,128)S(1)} collective-permute-done((f32[384,256]{1,0:T(8,128)S(1)}, f32[384,256]{1,0:T(8,128)S(1)}, u32[]{:S(2)}, u32[]{:S(2)}) %collective-permute-start.1) | collective-permute-done | bytes 393248 | tf_op jit(solution)/shard_map/ppermute | solution.py:23
  40.7 3.2 %slice.32 = bf16[1536,768]{1,0:T(8,128)(2,1)} slice(bf16[1536,1536]{1,0:T(8,128)(2,1)} %bitcast.68), slice={[0:1536], [768:1536]} | slice | bytes 4718592 | tf_op jit(solution)/shard_map/slice | solution.py:112
  61.6 24.9 %collective-permute-done.39.refs_1_ = bf16[1536,256]{1,0:T(8,128)(2,1)S(1)} collective-permute-done((bf16[1536,256]{1,0:T(8,128)(2,1)S(1)}, bf16[1536,256]{1,0:T(8,128)(2,1)S(1)}, u32[]{:S(2)}, u32[]{:S(2)}) %collective-permute-start.39) | collective-permute-done | bytes 786464 | tf_op jit(solution)/shard_map/ppermute | solution.py:18
  105.8 5.4 %collective-permute-done.12 = f16[384,512]{1,0:T(8,128)(2,1)S(1)} collective-permute-done((f16[384,512]{1,0:T(8,128)(2,1)S(1)}, f16[384,512]{1,0:T(8,128)(2,1)S(1)}, u32[]{:S(2)}, u32[]{:S(2)}) %collective-permute-start.12) | collective-permute-done | bytes 393248 | tf_op jit(solution)/shard_map/ppermute | solution.py:23
  111.2 3.5 %fusion = f16[384,768]{1,0:T(8,128)(2,1)S(1)} fusion(bf16[1536,384]{1,0:T(8,128)(2,1)S(1)} %copy-done.15, bf16[1536,768]{1,0:T(8,128)(2,1)} %collective-permute-done.17.refs_1_, f32[]{:T(128)} %bitcast.10), kind=kOutput, calls=%fused_computation.7 | convolution fusion | flops 906559488 | bytes 4128772 | tf_op jit(solution)/shard_map/dot_general | solution.py:32
  115.4 3.5 %fusion.1 = f16[384,768]{1,0:T(8,128)(2,1)S(1)} fusion(bf16[1536,384]{1,0:T(8,128)(2,1)S(1)} %copy-done.14, bf16[1536,768]{1,0:T(8,128)(2,1)} %collective-permute-done.17.refs_1_, f32[]{:T(128)} %bitcast.10), kind=kOutput, calls=%fused_computation.8 | convolution fusion | flops 906559488 | bytes 4128772 | tf_op jit(solution)/shard_map/dot_general | solution.py:32
  120.0 2.8 %fusion.19 = f32[384,768]{1,0:T(8,128)S(1)} fusion(bf16[1536,384]{1,0:T(8,128)(2,1)S(1)} %copy-done.12, bf16[1536,768]{1,0:T(8,128)(2,1)} %collective-permute-done.17.refs_1_), kind=kOutput, calls=%fused_computation.85 | convolution fusion | flops 905969664 | bytes 4718592 | tf_op jit(solution)/shard_map/dot_general | solution.py:32
  130.6 3.6 %collective-permute-done.21 = f16[384,768]{1,0:T(8,128)(2,1)S(1)} collective-permute-done((f16[384,768]{1,0:T(8,128)(2,1)S(1)}, f16[384,768]{1,0:T(8,128)(2,1)S(1)}, u32[]{:S(2)}, u32[]{:S(2)}) %collective-permute-start.21) | collective-permute-done | bytes 589856 | tf_op jit(solution)/shard_map/ppermute | solution.py:23
  143.4 3.5 %collective-permute-done.19 = f16[384,768]{1,0:T(8,128)(2,1)S(1)} collective-permute-done((f16[384,768]{1,0:T(8,128)(2,1)S(1)}, f16[384,768]{1,0:T(8,128)(2,1)S(1)}, u32[]{:S(2)}, u32[]{:S(2)}) %collective-permute-start.19) | collective-permute-done | bytes 589856 | tf_op jit(solution)/shard_map/ppermute | solution.py:23
  153.0 5.0 %collective-permute-done.33 = f16[384,512]{1,0:T(8,128)(2,1)S(1)} collective-permute-done((f16[384,512]{1,0:T(8,128)(2,1)S(1)}, f16[384,512]{1,0:T(8,128)(2,1)S(1)}, u32[]{:S(2)}, u32[]{:S(2)}) %collective-permute-start.33) | collective-permute-done | bytes 393248 | tf_op jit(solution)/shard_map/ppermute | solution.py:23
  163.5 3.1 %collective-permute-done.34 = f16[384,512]{1,0:T(8,128)(2,1)S(1)} collective-permute-done((f16[384,512]{1,0:T(8,128)(2,1)S(1)}, f16[384,512]{1,0:T(8,128)(2,1)S(1)}, u32[]{:S(2)}, u32[]{:S(2)}) %collective-permute-start.34) | collective-permute-done | bytes 393248 | tf_op jit(solution)/shard_map/ppermute | solution.py:23
  168.9 4.1 %collective-permute-done.37 = f16[384,512]{1,0:T(8,128)(2,1)S(1)} collective-permute-done((f16[384,512]{1,0:T(8,128)(2,1)S(1)}, f16[384,512]{1,0:T(8,128)(2,1)S(1)}, u32[]{:S(2)}, u32[]{:S(2)}) %collective-permute-start.37) | collective-permute-done | bytes 393248 | tf_op jit(solution)/shard_map/ppermute | solution.py:23
  181.9 7.7 %collective-permute-done.26 = f16[384,768]{1,0:T(8,128)(2,1)S(1)} collective-permute-done((f16[384,768]{1,0:T(8,128)(2,1)S(1)}, f16[384,768]{1,0:T(8,128)(2,1)S(1)}, u32[]{:S(2)}, u32[]{:S(2)}) %collective-permute-start.26) | collective-permute-done | bytes 589856 | tf_op jit(solution)/shard_map/ppermute | solution.py:23
  194.5 9.5 %collective-permute-done.27 = f16[384,768]{1,0:T(8,128)(2,1)S(1)} collective-permute-done((f16[384,768]{1,0:T(8,128)(2,1)S(1)}, f16[384,768]{1,0:T(8,128)(2,1)S(1)}, u32[]{:S(2)}, u32[]{:S(2)}) %collective-permute-start.27) | collective-permute-done | bytes 589856 | tf_op jit(solution)/shard_map/ppermute | solution.py:23
  211.4 4.6 %collective-permute-done.16.refs_9_ = bf16[384,512]{1,0:T(8,128)(2,1)S(1)} collective-permute-done((bf16[384,512]{1,0:T(8,128)(2,1)S(1)}, bf16[384,512]{1,0:T(8,128)(2,1)S(1)}, u32[]{:S(2)}, u32[]{:S(2)}) %collective-permute-start.16) | collective-permute-done | bytes 393248 | tf_op jit(solution)/shard_map/ppermute | solution.py:23
  217.7 4.5 %collective-permute-done.20.refs_3_ = bf16[384,768]{1,0:T(8,128)(2,1)S(1)} collective-permute-done((bf16[384,768]{1,0:T(8,128)(2,1)S(1)}, bf16[384,768]{1,0:T(8,128)(2,1)S(1)}, u32[]{:S(2)}, u32[]{:S(2)}) %collective-permute-start.20) | collective-permute-done | bytes 589856 | tf_op jit(solution)/shard_map/ppermute | solution.py:23
  223.0 5.6 %collective-permute-done.23.refs_5_ = bf16[384,768]{1,0:T(8,128)(2,1)S(1)} collective-permute-done((bf16[384,768]{1,0:T(8,128)(2,1)S(1)}, bf16[384,768]{1,0:T(8,128)(2,1)S(1)}, u32[]{:S(2)}, u32[]{:S(2)}) %collective-permute-start.23) | collective-permute-done | bytes 589856 | tf_op jit(solution)/shard_map/ppermute | solution.py:23
  230.4 4.5 %collective-permute-done.28.refs_3_ = bf16[384,768]{1,0:T(8,128)(2,1)S(1)} collective-permute-done((bf16[384,768]{1,0:T(8,128)(2,1)S(1)}, bf16[384,768]{1,0:T(8,128)(2,1)S(1)}, u32[]{:S(2)}, u32[]{:S(2)}) %collective-permute-start.28) | collective-permute-done | bytes 589856 | tf_op jit(solution)/shard_map/ppermute | solution.py:23
  236.4 6.7 %shard_map.55.refs_0_ = f32[1536,1536]{1,0:T(8,128)S(1)} custom-call(s32[4]{0:T(128)S(1)} %pad_add_fusion.places_ref, bf16[1536,256]{1,0:T(8,128)(2,1)S(1)} %copy-done.3, bf16[384,256]{1,0:T(8,128)(2,1)S(1)} %divide_convert_fusion.11.refs_1_, bf16[384,256]{1,0:T(8,128)(2,1)S(1)} %collective-permute-done.3.refs_2_, ...), custom_call_target="tpu_custom_call" | custom-call | tf_op jit(solution)/shard_map/pallas_call | solution.py:81
  243.1 7.6 %shard_map.56.refs_0_ = f32[1536,1536]{1,0:T(8,128)S(1)} custom-call(s32[4]{0:T(128)S(1)} %pad_add_fusion.places_ref, f32[1536,1536]{1,0:T(8,128)S(1)} %shard_map.55.refs_0_, bf16[1536,768]{1,0:T(8,128)(2,1)} %collective-permute-done.17.refs_1_, bf16[384,768]{1,0:T(8,128)(2,1)S(1)} %divide_convert_fusion.3.refs_2_, ...), custom_call_target="tpu_custom_call" | custom-call | tf_op jit(solution)/shard_map/pallas_call | solution.py:81
  252.6 6.5 %shard_map.57.refs_0_ = f32[1536,1536]{1,0:T(8,128)S(1)} custom-call(s32[4]{0:T(128)S(1)} %pad_add_fusion.places_ref, f32[1536,1536]{1,0:T(8,128)S(1)} %shard_map.56.refs_0_, bf16[1536,768]{1,0:T(8,128)(2,1)S(1)} %collective-permute-done.24.refs_1_, bf16[384,768]{1,0:T(8,128)(2,1)S(1)} %divide_convert_fusion.1.refs_2_, bf16[384,768]{1,0:T(8,128)(2,1)S(1)} %copy-done.5, ...), custom_call_target="tpu_custom_call" | custom-call | tf_op jit(solution)/shard_map/pallas_call | solution.py:81
  260.9 5.9 %shard_map.58.refs_0_ = f32[1536,1536]{1,0:T(8,128)S(1)} custom-call(s32[4]{0:T(128)S(1)} %pad_add_fusion.places_ref, f32[1536,1536]{1,0:T(8,128)S(1)} %shard_map.57.refs_0_, bf16[1536,512]{1,0:T(8,128)(2,1)S(1)} %collective-permute-done.32.refs_1_, bf16[384,512]{1,0:T(8,128)(2,1)S(1)} %divide_convert_fusion.5.refs_2_, bf16[384,512]{1,0:T(8,128)(2,1)S(1)} %copy-done.9, ...), custom_call_target="tpu_custom_call" | custom-call | tf_op jit(solution)/shard_map/pallas_call | solution.py:81
  266.9 7.2 %shard_map.59 = f32[18432,128]{1,0:T(8,128)} custom-call(s32[4]{0:T(128)S(1)} %pad_add_fusion.places_ref, f32[1536,1536]{1,0:T(8,128)S(1)} %shard_map.58.refs_0_, bf16[1536,256]{1,0:T(8,128)(2,1)S(1)} %copy-done.1, bf16[384,256]{1,0:T(8,128)(2,1)S(1)} %divide_convert_fusion.9.refs_2_, bf16[384,256]{1,0:T(8,128)(2,1)S(1)} %collective-permute-done.42.refs_3_, ...), custom_call_target="tpu_custom_call" | custom-call | tf_op jit(solution)/shard_map/pallas_call | solution.py:81
  (198 shorter events, 123.9 us)
Async XLA Ops:
  2.2 19.3 %collective-permute-start = (bf16[1536,256]{1,0:T(8,128)(2,1)}, bf16[1536,256]{1,0:T(8,128)(2,1)S(1)}, u32[]{:S(2)}, u32[]{:S(2)}) collective-permute-start(bf16[1536,256]{1,0:T(8,128)(2,1)} %slice.35), channel_id=1, source_target_pairs={{7,0},{0,1},{1,2},{2,3},{3,4},{4,5},{5,6},{6,7},{15,8},{8,9},{9,10... | collective-permute-start | bytes 2359304 | tf_op jit(solution)/shard_map/ppermute | solution.py:18
  5.4 47.4 %collective-permute-start.7 = (bf16[1536,512]{1,0:T(8,128)(2,1)}, bf16[1536,512]{1,0:T(8,128)(2,1)S(1)}, u32[]{:S(2)}, u32[]{:S(2)}) collective-permute-start(bf16[1536,512]{1,0:T(8,128)(2,1)} %slice.29), channel_id=1, source_target_pairs={{7,0},{0,1},{1,2},{2,3},{3,4},{4,5},{5,6},{6,7},{15,8},{8,9},{9,10... | collective-permute-start | bytes 4718600 | tf_op jit(solution)/shard_map/ppermute | solution.py:18
  19.9 17.3 %collective-permute-start.9 = (f32[8,128]{1,0:T(8,128)S(1)}, f32[8,128]{1,0:T(8,128)S(1)}, u32[]{:S(2)}, u32[]{:S(2)}) collective-permute-start(f32[8,128]{1,0:T(8,128)S(1)} %broadcast_maximum_fusion), channel_id=1, source_target_pairs={{0,16},{8,24},{16,0},{24,8},{1,17},{9,25},{17,1},{25,9},{2,18},{10... | collective-permute-start | bytes 12296 | tf_op jit(solution)/shard_map/ppermute | solution.py:23
  34.9 17.9 %collective-permute-start.2 = (f32[384,256]{1,0:T(8,128)}, f32[384,256]{1,0:T(8,128)}, u32[]{:S(2)}, u32[]{:S(2)}) collective-permute-start(f32[384,256]{1,0:T(8,128)} %add.151), channel_id=1, source_target_pairs={{0,16},{8,24},{16,0},{24,8},{1,17},{9,25},{17,1},{25,9},{2,18},{10... | collective-permute-start | bytes 1179656 | tf_op jit(solution)/shard_map/ppermute | solution.py:23
  47.7 63.5 %collective-permute-start.17 = (bf16[1536,768]{1,0:T(8,128)(2,1)}, bf16[1536,768]{1,0:T(8,128)(2,1)}, u32[]{:S(2)}, u32[]{:S(2)}) collective-permute-start(bf16[1536,768]{1,0:T(8,128)(2,1)} %slice.32), channel_id=1, source_target_pairs={{7,0},{0,1},{1,2},{2,3},{3,4},{4,5},{5,6},{6,7},{15,8},{8,9},{9,10... | collective-permute-start | bytes 7077896 | tf_op jit(solution)/shard_map/ppermute | solution.py:18
  52.7 33.8 %collective-permute-start.39 = (bf16[1536,256]{1,0:T(8,128)(2,1)S(1)}, bf16[1536,256]{1,0:T(8,128)(2,1)S(1)}, u32[]{:S(2)}, u32[]{:S(2)}) collective-permute-start(bf16[1536,256]{1,0:T(8,128)(2,1)S(1)} %collective-permute-done.refs_0_), channel_id=1, source_target_pairs={{7,0},{0,1},{1,2},{2,3},{3,4},{4,5},{5,6},{6,7},{15,8},{8,9},{9,10... | collective-permute-start | bytes 2359304 | tf_op jit(solution)/shard_map/ppermute | solution.py:18
  56.5 42.5 %collective-permute-start.11 = (f16[384,512]{1,0:T(8,128)(2,1)S(1)}, f16[384,512]{1,0:T(8,128)(2,1)S(1)}, u32[]{:S(2)}, u32[]{:S(2)}) collective-permute-start(f16[384,512]{1,0:T(8,128)(2,1)S(1)} %fusion.4), channel_id=1, source_target_pairs={{0,8},{8,0},{16,24},{24,16},{1,9},{9,1},{17,25},{25,17},{2,10},{10... | collective-permute-start | bytes 1179656 | tf_op jit(solution)/shard_map/ppermute | solution.py:23
  60.0 40.4 %collective-permute-start.14 = (f16[384,512]{1,0:T(8,128)(2,1)S(1)}, f16[384,512]{1,0:T(8,128)(2,1)S(1)}, u32[]{:S(2)}, u32[]{:S(2)}) collective-permute-start(f16[384,512]{1,0:T(8,128)(2,1)S(1)} %fusion.5), channel_id=1, source_target_pairs={{0,16},{8,24},{16,0},{24,8},{1,17},{9,25},{17,1},{25,9},{2,18},{10... | collective-permute-start | bytes 1179656 | tf_op jit(solution)/shard_map/ppermute | solution.py:23
  95.1 42.5 %collective-permute-start.32 = (bf16[1536,512]{1,0:T(8,128)(2,1)S(1)}, bf16[1536,512]{1,0:T(8,128)(2,1)S(1)}, u32[]{:S(2)}, u32[]{:S(2)}) collective-permute-start(bf16[1536,512]{1,0:T(8,128)(2,1)S(1)} %collective-permute-done.7.refs_5_), channel_id=1, source_target_pairs={{7,0},{0,1},{1,2},{2,3},{3,4},{4,5},{5,6},{6,7},{15,8},{8,9},{9,10... | collective-permute-start | bytes 4718600 | tf_op jit(solution)/shard_map/ppermute | solution.py:18
  104.3 21.6 %collective-permute-start.15 = (f16[384,512]{1,0:T(8,128)(2,1)S(1)}, f16[384,512]{1,0:T(8,128)(2,1)S(1)}, u32[]{:S(2)}, u32[]{:S(2)}) collective-permute-start(f16[384,512]{1,0:T(8,128)(2,1)S(1)} %multiply_convert_fusion.6), channel_id=1, source_target_pairs={{0,8},{8,0},{16,24},{24,16},{1,9},{9,1},{17,25},{25,17},{2,10},{10... | collective-permute-start | bytes 1179656 | tf_op jit(solution)/shard_map/ppermute | solution.py:23
  125.6 47.5 %collective-permute-start.24 = (bf16[1536,768]{1,0:T(8,128)(2,1)}, bf16[1536,768]{1,0:T(8,128)(2,1)S(1)}, u32[]{:S(2)}, u32[]{:S(2)}) collective-permute-start(bf16[1536,768]{1,0:T(8,128)(2,1)} %collective-permute-done.17.refs_1_), channel_id=1, source_target_pairs={{7,0},{0,1},{1,2},{2,3},{3,4},{4,5},{5,6},{6,7},{15,8},{8,9},{9,10... | collective-permute-start | bytes 7077896 | tf_op jit(solution)/shard_map/ppermute | solution.py:18
  129.5 17.4 %collective-permute-start.19 = (f16[384,768]{1,0:T(8,128)(2,1)S(1)}, f16[384,768]{1,0:T(8,128)(2,1)S(1)}, u32[]{:S(2)}, u32[]{:S(2)}) collective-permute-start(f16[384,768]{1,0:T(8,128)(2,1)S(1)} %multiply_convert_fusion.3), channel_id=1, source_target_pairs={{0,16},{8,24},{16,0},{24,8},{1,17},{9,25},{17,1},{25,9},{2,18},{10... | collective-permute-start | bytes 1769480 | tf_op jit(solution)/shard_map/ppermute | solution.py:23
  139.0 19.0 %collective-permute-start.33 = (f16[384,512]{1,0:T(8,128)(2,1)S(1)}, f16[384,512]{1,0:T(8,128)(2,1)S(1)}, u32[]{:S(2)}, u32[]{:S(2)}) collective-permute-start(f16[384,512]{1,0:T(8,128)(2,1)S(1)} %fusion.6), channel_id=1, source_target_pairs={{0,8},{8,0},{16,24},{24,16},{1,9},{9,1},{17,25},{25,17},{2,10},{10... | collective-permute-start | bytes 1179656 | tf_op jit(solution)/shard_map/ppermute | solution.py:23
  140.5 19.7 %collective-permute-start.36 = (f16[384,512]{1,0:T(8,128)(2,1)S(1)}, f16[384,512]{1,0:T(8,128)(2,1)S(1)}, u32[]{:S(2)}, u32[]{:S(2)}) collective-permute-start(f16[384,512]{1,0:T(8,128)(2,1)S(1)} %fusion.7), channel_id=1, source_target_pairs={{0,16},{8,24},{16,0},{24,8},{1,17},{9,25},{17,1},{25,9},{2,18},{10... | collective-permute-start | bytes 1179656 | tf_op jit(solution)/shard_map/ppermute | solution.py:23
  146.9 61.3 %collective-permute-start.3 = (bf16[384,256]{1,0:T(8,128)(2,1)S(1)}, bf16[384,256]{1,0:T(8,128)(2,1)S(1)}, u32[]{:S(2)}, u32[]{:S(2)}) collective-permute-start(bf16[384,256]{1,0:T(8,128)(2,1)S(1)} %divide_convert_fusion.11.refs_1_), channel_id=1, source_target_pairs={{0,8},{8,0},{16,24},{24,16},{1,9},{9,1},{17,25},{25,17},{2,10},{10... | collective-permute-start | bytes 589832 | tf_op jit(solution)/shard_map/ppermute | solution.py:23
  151.7 57.5 %collective-permute-start.6 = (bf16[384,256]{1,0:T(8,128)(2,1)S(1)}, bf16[384,256]{1,0:T(8,128)(2,1)S(1)}, u32[]{:S(2)}, u32[]{:S(2)}) collective-permute-start(bf16[384,256]{1,0:T(8,128)(2,1)S(1)} %divide_convert_fusion.10.refs_3_), channel_id=1, source_target_pairs={{0,16},{8,24},{16,0},{24,8},{1,17},{9,25},{17,1},{25,9},{2,18},{10... | collective-permute-start | bytes 589832 | tf_op jit(solution)/shard_map/ppermute | solution.py:23
  166.6 43.0 %collective-permute-start.13 = (bf16[384,512]{1,0:T(8,128)(2,1)S(1)}, bf16[384,512]{1,0:T(8,128)(2,1)S(1)}, u32[]{:S(2)}, u32[]{:S(2)}) collective-permute-start(bf16[384,512]{1,0:T(8,128)(2,1)S(1)} %divide_convert_fusion.7.refs_6_), channel_id=1, source_target_pairs={{0,8},{8,0},{16,24},{24,16},{1,9},{9,1},{17,25},{25,17},{2,10},{10... | collective-permute-start | bytes 1179656 | tf_op jit(solution)/shard_map/ppermute | solution.py:23
  208.2 20.5 %collective-permute-start.23 = (bf16[384,768]{1,0:T(8,128)(2,1)S(1)}, bf16[384,768]{1,0:T(8,128)(2,1)S(1)}, u32[]{:S(2)}, u32[]{:S(2)}) collective-permute-start(bf16[384,768]{1,0:T(8,128)(2,1)S(1)} %divide_convert_fusion.2.refs_4_), channel_id=1, source_target_pairs={{0,16},{8,24},{16,0},{24,8},{1,17},{9,25},{17,1},{25,9},{2,18},{10... | collective-permute-start | bytes 1769480 | tf_op jit(solution)/shard_map/ppermute | solution.py:23
  209.2 25.7 %collective-permute-start.28 = (bf16[384,768]{1,0:T(8,128)(2,1)S(1)}, bf16[384,768]{1,0:T(8,128)(2,1)S(1)}, u32[]{:S(2)}, u32[]{:S(2)}) collective-permute-start(bf16[384,768]{1,0:T(8,128)(2,1)S(1)} %divide_convert_fusion.1.refs_2_), channel_id=1, source_target_pairs={{0,8},{8,0},{16,24},{24,16},{1,9},{9,1},{17,25},{25,17},{2,10},{10... | collective-permute-start | bytes 1769480 | tf_op jit(solution)/shard_map/ppermute | solution.py:23
  209.6 41.1 %collective-permute-start.31 = (bf16[384,768]{1,0:T(8,128)(2,1)S(1)}, bf16[384,768]{1,0:T(8,128)(2,1)S(1)}, u32[]{:S(2)}, u32[]{:S(2)}) collective-permute-start(bf16[384,768]{1,0:T(8,128)(2,1)S(1)} %divide_convert_fusion.refs_4_), channel_id=1, source_target_pairs={{0,16},{8,24},{16,0},{24,8},{1,17},{9,25},{17,1},{25,9},{2,18},{10... | collective-permute-start | bytes 1769480 | tf_op jit(solution)/shard_map/ppermute | solution.py:23
  216.0 43.2 %collective-permute-start.35 = (bf16[384,512]{1,0:T(8,128)(2,1)S(1)}, bf16[384,512]{1,0:T(8,128)(2,1)S(1)}, u32[]{:S(2)}, u32[]{:S(2)}) collective-permute-start(bf16[384,512]{1,0:T(8,128)(2,1)S(1)} %divide_convert_fusion.5.refs_2_), channel_id=1, source_target_pairs={{0,8},{8,0},{16,24},{24,16},{1,9},{9,1},{17,25},{25,17},{2,10},{10... | collective-permute-start | bytes 1179656 | tf_op jit(solution)/shard_map/ppermute | solution.py:23
  222.2 37.7 %collective-permute-start.38 = (bf16[384,512]{1,0:T(8,128)(2,1)S(1)}, bf16[384,512]{1,0:T(8,128)(2,1)}, u32[]{:S(2)}, u32[]{:S(2)}) collective-permute-start(bf16[384,512]{1,0:T(8,128)(2,1)S(1)} %divide_convert_fusion.4.refs_4_), channel_id=1, source_target_pairs={{0,16},{8,24},{16,0},{24,8},{1,17},{9,25},{17,1},{25,9},{2,18},{10... | collective-permute-start | bytes 1179656 | tf_op jit(solution)/shard_map/ppermute | solution.py:23
  228.7 38.2 %collective-permute-start.42 = (bf16[384,256]{1,0:T(8,128)(2,1)S(1)}, bf16[384,256]{1,0:T(8,128)(2,1)S(1)}, u32[]{:S(2)}, u32[]{:S(2)}) collective-permute-start(bf16[384,256]{1,0:T(8,128)(2,1)S(1)} %divide_convert_fusion.9.refs_2_), channel_id=1, source_target_pairs={{0,8},{8,0},{16,24},{24,16},{1,9},{9,1},{17,25},{25,17},{2,10},{10... | collective-permute-start | bytes 589832 | tf_op jit(solution)/shard_map/ppermute | solution.py:23
  235.7 31.2 %collective-permute-start.45 = (bf16[384,256]{1,0:T(8,128)(2,1)S(1)}, bf16[384,256]{1,0:T(8,128)(2,1)}, u32[]{:S(2)}, u32[]{:S(2)}) collective-permute-start(bf16[384,256]{1,0:T(8,128)(2,1)S(1)} %divide_convert_fusion.8.refs_4_), channel_id=1, source_target_pairs={{0,16},{8,24},{16,0},{24,8},{1,17},{9,25},{17,1},{25,9},{2,18},{10... | collective-permute-start | bytes 589832 | tf_op jit(solution)/shard_map/ppermute | solution.py:23
  (45 other events, 420.6 us)
